TPU v7x, 32 devices: a whole 2x2x4 slice. The times are simulated.
32 devices in a mesh: traj: 4 (over z), lon: 8 (over y, x, core).
Axes of the slice: x: 2, y: 2, z: 4, core: 2. Of those that a mesh axis runs over, the one named last changes fastest.
Arguments:
- states: float32 [4, 78, 16, 1024], P('traj', None, None, 'lon')
- obs_index: int32 [4, 2048], P('traj', 'lon'), may hold values from 0 to 16383, as said below
- obs_values: float32 [4, 78, 2048], P('traj', None, 'lon'), may hold values from -8 to 8
- first_weight: bfloat16 [256, 2106], replicated, may hold values from -0.125 to 0.125
- first_bias: float32 [256], replicated, may hold values from -4 to 4
- second_weight: bfloat16 [234, 2304], replicated, may hold values from -0.125 to 0.125
Outputs:
- updated: float32 [4, 78, 16, 1024], P('traj', None, None, 'lon')
Inputs may be any that keep to these rules, and one draw needn't show every extreme that they name: Entries k of obs_index[t] with k // 256 = j lie in longitude columns j * 128 to (j + 1) * 128 - 1; the cells of one state are distinct.
All inputs are finite; a program needn't handle non-finite values.
Results may differ from a plain program's by a relative error of at most 0.0028.
Values may be sent and summed in bfloat16 or wider, within the bound.
A program may use at most 128 MiB of HBM per device.

v0:
```python
import functools

import jax
import jax.numpy as jnp
from jax import lax
from jax.experimental import pallas as pl
from jax.experimental.pallas import tpu as pltpu
from jax.sharding import PartitionSpec as P

STEPS = 2
F32 = jnp.float32
BF16 = jnp.bfloat16
LANES = 128
HALF = 64
PIECE = 16
MESH = pl.DeviceIdType.MESH


def lane_of(shape):
    return lax.broadcasted_iota(jnp.int32, shape, len(shape) - 1)


def turned(value, by):
    by = by % LANES
    return value if by == 0 else pltpu.roll(value, by, len(value.shape) - 1)


def pack_pair(lane, low, high):
    return jnp.where(lane < HALF, low, turned(high, HALF))


def pack_tails(lane, cols):
    out = jnp.zeros_like(cols[0])
    for i, col in enumerate(cols):
        out = jnp.where(lane // PIECE == i, turned(col, PIECE * i - HALF), out)
    return out


def kernel(
    nt, nl, nvar, rows, cols, hid,
    x_ref, loc_ref, val_ref, w1_ref, b1_ref, w2_ref, out_ref,
    xn, xt, base, quot, obs3, bt, pn, pb, rn, rb, en, eb, nu, xb, x3, acc, h3, score,
    qs, rq, st, red1, sum1, red2,
    bar_n_s, bar_n_r, bar_b_s, bar_b_r, edge_s, edge_n_r, edge_b_r, ret_s, ret_r,
    r1_s, r1_r, r2_s, r2_r,
):
    t = lax.axis_index("traj")
    b = lax.axis_index("lon")
    cw = cols // nt
    halo = 2 * STEPS
    ext = cw + 2 * halo
    mt = 5 * cw // 8
    tiles = mt + 6
    count = nt * rows * cols * nl
    lane = lane_of((rows, LANES))
    row = lax.broadcasted_iota(jnp.int32, (rows, LANES), 0)

    def dev(tt, bb):
        return {"traj": lax.rem(tt, nt), "lon": lax.rem(bb, nl)}

    barrier = pltpu.get_barrier_semaphore()
    partners = 0
    for db in range(nl):
        for dt in range(nt):
            near = db in (0, 1, nl - 1)
            if (db or dt) and (near or dt == 0):
                pl.semaphore_signal(barrier, inc=1, device_id=dev(t + dt, b + db), device_id_type=MESH)
                partners += 1

    xn[0 : nvar * rows, :] = x_ref[...]
    xn[nvar * rows :, :] = jnp.zeros((LANES * rows - nvar * rows, LANES), F32)

    def flip(r, c):
        xt[pl.ds(r, cols, stride=rows), :] = xn[pl.ds(r, LANES, stride=rows), :].T
        return c

    lax.fori_loop(0, rows, flip, 0)

    def squares(ref, first, n):
        def one(i, c):
            v = ref[pl.ds(first + i * 32, 32), :]
            return c + v * v

        s = lax.fori_loop(0, n // 32, one, jnp.zeros((32, LANES), F32))
        return s[0:8] + s[8:16] + s[16:24] + s[24:32]

    def reduced(step, part, first):
        sum1[step, 0] = part
        copies = []
        for i in range(1, nt):
            cp = pltpu.make_async_remote_copy(
                sum1.at[step, 0], red1.at[step, i], r1_s.at[step, i], r1_r.at[step, i],
                device_id=dev(t + i, b), device_id_type=MESH)
            cp.start()
            copies.append(cp)
        tot = part
        for i in range(1, nt):
            copies[i - 1].wait()
            tot = tot + red1[step, i]
        sum1[step, 1] = tot
        copies = []
        for i in range(1, nl):
            cp = pltpu.make_async_remote_copy(
                sum1.at[step, 1], red2.at[step, i], r2_s.at[step, i], r2_r.at[step, i],
                device_id=dev(t, b + i), device_id_type=MESH)
            cp.start()
            copies.append(cp)
        for i in range(1, nl):
            copies[i - 1].wait()
            tot = tot + red2[step, i]
        moment = jnp.sum(tot, axis=0, keepdims=True) / count
        return jnp.broadcast_to(1.0 / jnp.sqrt(moment + 1e-06), (rows, LANES))

    part = squares(xt, 0, cols * rows)
    pl.semaphore_wait(barrier, partners)
    scale = reduced(0, part, True)

    def pack_all(get, dest):
        zero = jnp.zeros((3, rows, LANES), BF16)
        dest[1, 0:3] = zero
        dest[nt, tiles - 3 :] = zero

        def sub(k, carry):
            def pair(j, c):
                dest[k + 1, 3 + j] = pack_pair(lane, get(k * cw + j), get(k * cw + j + cw // 2)).astype(BF16)
                return c

            lax.fori_loop(0, cw // 2, pair, 0, unroll=2)

            def tail(j, c):
                dest[k + 1, 3 + cw // 2 + j] = pack_tails(
                    lane, [get(k * cw + j + cw // 8 * i) for i in range(8)]).astype(BF16)
                return c

            lax.fori_loop(0, cw // 8, tail, 0)
            for first, slot, at in ((k * cw, k, tiles - 3), (k * cw + cw - halo, k + 2, 0)):
                four = [get(first + i) for i in range(4)]
                dest[slot, at] = pack_pair(lane, four[0], four[2]).astype(BF16)
                dest[slot, at + 1] = pack_pair(lane, four[1], four[3]).astype(BF16)
                dest[slot, at + 2] = pack_tails(lane, four).astype(BF16)
            return carry

        lax.fori_loop(0, nt, sub, 0)

    def send_all(src, dst, edge, s_sem, r_sem, e_sem, f):
        copies = []
        for i in range(1, nt):
            k = lax.rem(t + i, nt)
            cp = pltpu.make_async_remote_copy(
                src.at[k + 1], dst.at[t], s_sem.at[i], r_sem.at[t],
                device_id=dev(k, b), device_id_type=MESH)
            cp.start()
            copies.append(cp)
        right = pltpu.make_async_remote_copy(
            src.at[nt + 1, 0:3], edge.at[t], edge_s.at[f, 0], e_sem.at[t],
            device_id=dev(0, b + 1), device_id_type=MESH)
        left = pltpu.make_async_remote_copy(
            src.at[0, tiles - 3 : tiles], edge.at[t], edge_s.at[f, 1], e_sem.at[t],
            device_id=dev(nt - 1, b + nl - 1), device_id_type=MESH)
        right.start()
        left.start()
        dst[t] = src[t + 1]
        return copies + [right, left]

    def receive(src, dst, edge, s_sem, r_sem, e_sem, f):
        for i in range(1, nt):
            k = lax.rem(t + i, nt)
            pltpu.make_async_remote_copy(
                src.at[k + 1], dst.at[k], s_sem.at[i], r_sem.at[k],
                device_id=dev(k, b), device_id_type=MESH).wait_recv()

        def edges(at, side):
            for k in range(nt):
                pltpu.make_async_remote_copy(
                    src.at[0, 0:3], edge.at[k], edge_s.at[f, 0], e_sem.at[k],
                    device_id=dev(0, b + 1), device_id_type=MESH).wait_recv()
                dst[k, at : at + 3] = edge[k]

        @pl.when(t == 0)
        def _():
            edges(0, 1)

        @pl.when(t == nt - 1)
        def _():
            edges(tiles - 3, -1)

    def unpack_all(src, put):
        def state(s, carry):
            def tile(j):
                return src[s, j].astype(F32)

            for at, first in ((0, 0), (tiles - 3, cw + halo)):
                pairs = [tile(at), tile(at + 1)]
                tail = tile(at + 2)
                for i in range(4):
                    a = turned(pairs[i % 2], HALF * (i // 2))
                    put(s, first + i, jnp.where(lane < HALF, a, turned(tail, HALF - PIECE * i)))
            unpack_main(lambda j: tile(3 + j), lambda c, v: put(s, c + halo, v))
            return carry

        lax.fori_loop(0, nt, state, 0)

    def unpack_main(tile, put):
        for i in range(8):
            def one(j, c, i=i):
                at = i * (cw // 8) + j
                a = turned(tile(at % (cw // 2) if isinstance(at, int) else at - (i // 4) * (cw // 2)), HALF * (i // 4))
                put(at, jnp.where(lane < HALF, a, turned(tile(cw // 2 + j), HALF - PIECE * i)))
                return c

            lax.fori_loop(0, cw // 8, one, 0, unroll=2)

    pack_all(lambda c: xt[pl.ds(c * rows, rows), :] * scale, pn)
    sent_n = send_all(pn, rn, en, bar_n_s, bar_n_r, edge_n_r, 0)

    vals = jnp.concatenate([val_ref[...], jnp.ones((8, val_ref.shape[1]), F32)], 0) if nvar % 8 == 0 else None
    if vals is None:
        obs_rows = val_ref.shape[0]
        obs3[0, 0:obs_rows] = val_ref[...]
        obs3[0, obs_rows:] = jnp.ones((LANES - obs_rows, val_ref.shape[1]), F32)
    else:
        obs3[0, 0 : nvar + 8] = vals
        obs3[0, nvar + 8 :] = jnp.zeros((LANES - nvar - 8, val_ref.shape[1]), F32)
    full = obs3[0]
    high = full.astype(BF16)
    rest = full - high.astype(F32)
    mid = rest.astype(BF16)
    low = (rest - mid.astype(F32)).astype(BF16)
    three = jnp.concatenate([high, mid, low], 0)
    loc = loc_ref[...]

    def observe(r, c):
        cell = lax.broadcasted_iota(jnp.int32, (cols, loc.shape[1]), 0) + r * cols
        hot = jnp.where(cell == loc, 1.0, 0.0).astype(BF16)
        o = lax.dot_general(three, hot, (((1,), (1,)), ((), ())), preferred_element_type=F32)
        o = o[0:LANES] + o[LANES : 2 * LANES] + o[2 * LANES :]
        seen = o[nvar : nvar + 1, :] > 0.5
        x = xn[pl.ds(r, LANES, stride=rows), :]
        g = jnp.where(seen, 0.5 * (o - x), 0.0)
        base[pl.ds(r, LANES, stride=rows), :] = jnp.where(seen, 0.5 * (x + g + o), x)
        quot[pl.ds(r, 1), :] = jnp.where(seen, 0.25, 0.5)
        bt[pl.ds(r, cols, stride=rows), :] = (x + g).T
        return c

    lax.fori_loop(0, rows, observe, 0)
    pack_all(lambda c: bt[pl.ds(c * rows, rows), :], pb)
    sent_b = send_all(pb, rb, eb, bar_b_s, bar_b_r, edge_b_r, 1)

    nu[0] = jnp.zeros(nu.shape[1:], F32)
    nu[nt + 1] = jnp.zeros(nu.shape[1:], F32)
    receive(pn, rn, en, bar_n_s, bar_n_r, edge_n_r, 0)

    def put_n(s, c, v):
        nu[s + 1, c] = v

    unpack_all(rn, put_n)

    def spread(dest, c, tile_list):
        n = len(tile_list)
        for i, v in enumerate(tile_list):
            up = jnp.where(row == 0, 0.0, pltpu.roll(v, 1, 0))
            down = jnp.where(row == rows - 1, 0.0, pltpu.roll(v, rows - 1, 0))
            for a, piece in enumerate((up, v, down)):
                dest[c, :, a * n * LANES + i * LANES : a * n * LANES + (i + 1) * LANES] = piece.astype(BF16)

    wide = 2 * LANES
    two = 2 * nvar - LANES

    def network(width):
        score[...] = jnp.zeros(score.shape, F32)

        def state(s, carry):
            def window(c, k):
                before, here, after = nu[s, c], nu[s + 1, c], nu[s + 2, c]
                moved = turned(here, nvar)
                first = jnp.where(lane < nvar, before, moved)
                last = jnp.where(lane < two, moved, jnp.where(lane < two + nvar, turned(after, two), 0.0))
                spread(x3, c, [first, last])
                return k

            lax.fori_loop(0, width, window, 0, unroll=2)
            wid = width - 2
            lhs = jnp.concatenate(
                [x3[i : i + wid].reshape(wid * rows, 3 * wide) for i in range(3)], 1)
            acc[0 : wid * rows, :] = jnp.dot(lhs, w1_ref[...], preferred_element_type=F32)
            bias = jnp.broadcast_to(b1_ref[...], (rows, hid))

            def activate(c, k):
                v = acc[pl.ds(c * rows, rows), :] + bias
                v = v / (1.0 + jnp.exp(-v))
                v = v.astype(BF16).astype(F32)
                spread(h3, c, [v[:, i * LANES : (i + 1) * LANES] for i in range(hid // LANES)])
                return k

            lax.fori_loop(0, wid, activate, 0, unroll=2)
            wid = width - 4
            lhs = jnp.concatenate(
                [h3[i : i + wid].reshape(wid * rows, 3 * hid) for i in range(3)], 1)
            acc[0 : wid * rows, :] = jnp.dot(lhs, w2_ref[...], preferred_element_type=F32)

            def share(c, k):
                c0 = acc[pl.ds(c * rows, rows), 0:LANES]
                c1 = acc[pl.ds(c * rows, rows), LANES : 2 * LANES]
                mid_part = jnp.where(lane < LANES - nvar, turned(c0, -nvar), turned(c1, -nvar))
                score[s, c] += c0
                score[s + 1, c] += mid_part
                score[s + 2, c] += turned(c1, -two)
                return k

            lax.fori_loop(0, wid, share, 0, unroll=2)
            return carry

        lax.fori_loop(0, nt, state, 0)

    def give_back(step, off):
        def state(s, carry):
            def get(c):
                return score[s + 1, c + off]

            def pair(j, c):
                qs[step, s, j] = pack_pair(lane, get(j), get(j + cw // 2)).astype(BF16)
                return c

            lax.fori_loop(0, cw // 2, pair, 0, unroll=2)

            def tail(j, c):
                qs[step, s, cw // 2 + j] = pack_tails(
                    lane, [get(j + cw // 8 * i) for i in range(8)]).astype(BF16)
                return c

            lax.fori_loop(0, cw // 8, tail, 0)
            return carry

        lax.fori_loop(0, nt, state, 0)
        copies = []
        for i in range(1, nt):
            k = lax.rem(t + i, nt)
            cp = pltpu.make_async_remote_copy(
                qs.at[step, k], rq.at[step, t], ret_s.at[step, i], ret_r.at[step, t],
                device_id=dev(k, b), device_id_type=MESH)
            cp.start()
            copies.append(cp)
        rq[step, t] = qs[step, t]
        return copies

    def take_back(step):
        for i in range(1, nt):
            k = lax.rem(t + i, nt)
            pltpu.make_async_remote_copy(
                qs.at[step, k], rq.at[step, k], ret_s.at[step, i], ret_r.at[step, k],
                device_id=dev(k, b), device_id_type=MESH).wait_recv()

        def band(k, carry):
            def put(c, v):
                st[pl.ds((k * cw + c) * rows, rows), :] = v

            unpack_main(lambda j: rq[step, k, j].astype(F32), put)
            return carry

        lax.fori_loop(0, nt, band, 0)

    network(ext)
    sent_1 = give_back(0, 2)

    receive(pb, rb, eb, bar_b_s, bar_b_r, edge_b_r, 1)

    def put_x(s, c, v):
        xb[s, c] = v

    unpack_all(rb, put_x)

    def advance(s, total):
        def one(c, k):
            v = xb[s, c + 2] + 0.5 * score[s + 1, c]
            nu[s + 1, c] = v
            return k

        lax.fori_loop(0, ext - 4, one, 0, unroll=2)

        def sq(c, k):
            v = nu[s + 1, c + 2]
            return k + v * v

        return lax.fori_loop(0, cw, sq, total, unroll=2)

    total = lax.fori_loop(0, nt, advance, jnp.zeros((rows, LANES), F32))
    part = total[0:8]
    for i in range(1, rows // 8):
        part = part + total[8 * i : 8 * i + 8]
    scale = reduced(1, part, False)

    def rescale(s, carry):
        def one(c, k):
            nu[s + 1, c] = (nu[s + 1, c] * scale).astype(BF16).astype(F32)
            return k

        return lax.fori_loop(0, ext - 4, one, carry, unroll=2)

    lax.fori_loop(0, nt, rescale, 0)
    network(ext - 4)
    sent_2 = give_back(1, 0)

    take_back(0)

    def add_first(r, c):
        v = st[pl.ds(r, cols, stride=rows), :].T
        at = pl.ds(r, LANES, stride=rows)
        base[at, :] = base[at, :] + quot[pl.ds(r, 1), :] * v
        return c

    lax.fori_loop(0, rows, add_first, 0)
    take_back(1)

    def add_second(r, c):
        v = st[pl.ds(r, cols, stride=rows), :].T
        at = pl.ds(r, LANES, stride=rows)
        base[at, :] = base[at, :] + 0.5 * v
        return c

    lax.fori_loop(0, rows, add_second, 0)
    out_ref[...] = base[0 : nvar * rows, :]
    for cp in sent_n + sent_b + sent_1 + sent_2:
        cp.wait_send()


def body(states, obs_index, obs_values, first_weight, first_bias, second_weight):
    nt, nl = lax.axis_size("traj"), lax.axis_size("lon")
    _, nvar, rows, cols = states.shape
    hid = first_bias.shape[0]
    band = lax.axis_index("lon")
    lon_total = cols * nl
    loc = obs_index // lon_total * cols + obs_index % lon_total - band * cols
    wide = 2 * LANES
    w1 = first_weight.reshape(hid, 3, 3, 3 * nvar)
    w1 = jnp.pad(w1, ((0, 0), (0, 0), (0, 0), (0, wide - 3 * nvar)))
    w1 = w1.transpose(2, 1, 3, 0).reshape(9 * wide, hid)
    w2 = jnp.pad(second_weight, ((0, wide - 3 * nvar), (0, 0))).reshape(wide, 3, 3, hid)
    w2 = w2.transpose(2, 1, 3, 0).reshape(9 * hid, wide)
    cw = cols // nt
    ext = cw + 4 * STEPS
    mt = 5 * cw // 8
    tiles = mt + 6
    nobs = obs_values.shape[2]
    dma = pltpu.SemaphoreType.DMA
    vm = pltpu.VMEM
    big = LANES * rows
    scratch = [
        vm((big, LANES), F32), vm((cols * rows, LANES), F32), vm((big, LANES), F32), vm((rows, LANES), F32),
        vm((1, LANES, nobs), F32), vm((cols * rows, LANES), F32),
        vm((nt + 2, tiles, rows, LANES), BF16), vm((nt + 2, tiles, rows, LANES), BF16),
        vm((nt, tiles, rows, LANES), BF16), vm((nt, tiles, rows, LANES), BF16),
        vm((nt, 3, rows, LANES), BF16), vm((nt, 3, rows, LANES), BF16),
        vm((nt + 2, ext, rows, LANES), F32), vm((nt, ext, rows, LANES), F32),
        vm((ext, rows, 3 * wide), BF16), vm((ext * rows, wide), F32), vm((ext, rows, 3 * hid), BF16),
        vm((nt + 2, ext - 4, rows, LANES), F32),
        vm((STEPS, nt, mt, rows, LANES), BF16), vm((STEPS, nt, mt, rows, LANES), BF16),
        vm((cols * rows, LANES), F32),
        vm((STEPS, nt, 8, LANES), F32), vm((STEPS, 2, 8, LANES), F32), vm((STEPS, nl, 8, LANES), F32),
        dma((nt,)), dma((nt,)), dma((nt,)), dma((nt,)), dma((2, 2)), dma((nt,)), dma((nt,)),
        dma((STEPS, nt)), dma((STEPS, nt)),
        dma((STEPS, nt)), dma((STEPS, nt)), dma((STEPS, nl)), dma((STEPS, nl)),
    ]
    out = pl.pallas_call(
        functools.partial(kernel, nt, nl, nvar, rows, cols, hid),
        out_shape=jax.ShapeDtypeStruct((nvar * rows, cols), F32),
        in_specs=[pl.BlockSpec(memory_space=vm)] * 6,
        out_specs=pl.BlockSpec(memory_space=vm),
        scratch_shapes=scratch,
        compiler_params=pltpu.CompilerParams(
            collective_id=0, has_side_effects=True, vmem_limit_bytes=60 << 20),
    )(states.reshape(nvar * rows, cols), loc, obs_values[0], w1, first_bias.reshape(1, hid), w2)
    return out.reshape(1, nvar, rows, cols)


def solution(mesh):
    placed = (P("traj", None, None, "lon"), P("traj", "lon"), P("traj", None, "lon"), P(), P(), P())
    return jax.shard_map(
        body, mesh=mesh, in_specs=placed, out_specs=P("traj", None, None, "lon"), check_vma=False
    )
```

profile of v0, /device:TPU:0, one launch (start us, length us, event | category | flops | bytes accessed | tf_op | source)
XLA Modules:
  0.0 135.1 jit_solution(14891799099378637062)
XLA Ops:
  0.0 1.6 %copy.10 = bf16[234,2304]{0,1:T(8,128)(2,1)S(1)} copy(bf16[234,2304]{1,0:T(8,128)(2,1)} %param.11) | data formatting | bytes 2156544 | tf_op args[5]
  1.6 0.2 pad.9
  1.8 0.0 copy-start
  1.8 1.1 copy.11
  2.9 0.5 copy-done
  3.4 0.2 reshape.22
  3.7 0.1 copy.9
  3.8 0.0 copy-start.1
  3.8 0.0 copy-start.2
  3.8 1.1 pad.8
  4.9 0.0 copy-done.1
  4.9 0.6 copy.14
  5.5 0.0 copy-done.2
  5.5 0.6 fusion.1.loc_ref
  6.1 127.0 %shard_map.64 = f32[1248,128]{1,0:T(8,128)} custom-call(f32[1248,128]{1,0:T(8,128)} %bitcast.19, s32[1,256]{1,0:T(1,128)} %fusion.1.loc_ref, f32[78,256]{1,0:T(8,128)} %bitcast.20, bf16[2304,256]{1,0:T(8,128)(2,1)} %bitcast.15, f32[1,256]{1,0:T(1,128)} %bitcast.21, bf16[2304,256]{1,0:T(8,128)(2,1)} %bitcast.16), custom_call_target="tpu_custom_call" | custom-call | tf_op jit(solution)/shard_map/pallas_call | solution.py:463
  133.1 2.0 %copy.16 = f32[1,78,16,128]{3,2,1,0:T(8,128)} copy(f32[1,78,16,128]{3,2,1,0:T(8,128)} %bitcast.18) | data formatting | bytes 1277952
Async XLA Ops:
  1.8 1.7 %copy-start = (bf16[256,2106]{0,1:T(8,128)(2,1)S(1)}, bf16[256,2106]{0,1:T(8,128)(2,1)}, u32[]{:S(2)}) copy-start(bf16[256,2106]{0,1:T(8,128)(2,1)} %param.9) | copy-start | bytes 3234820
  3.8 1.1 copy-start.1
  3.8 1.8 %copy-start.2 = (s32[1,256]{1,0:T(1,128)S(1)}, s32[1,256]{1,0:T(1,128)}, u32[]{:S(2)}) copy-start(s32[1,256]{1,0:T(1,128)} %param.7) | copy-start | bytes 3076
where the time goes:
time: 135 us
  Pallas kernels  127 us (94%)
  local copies, waits for them, and re-layouts  7.45 us (6%)
    pallas_call x1, Pallas kernels, body(): pl.pallas_call(functools.partial(kernel, nt, nl, nvar, rows, cols, hid),...  127 us
    unnamed x9, local copies, waits for them, and re-layouts  4.67 us

commit v1 on v0

--- a/solution.py
+++ b/solution.py
@@ -13,6 +13,7 @@
 LANES = 128
 HALF = 64
 PIECE = 16
+GROUP = 4
 MESH = pl.DeviceIdType.MESH
 
 
@@ -25,12 +26,13 @@
     return value if by == 0 else pltpu.roll(value, by, len(value.shape) - 1)
 
 
-def pack_pair(lane, low, high):
-    return jnp.where(lane < HALF, low, turned(high, HALF))
-
-
-def pack_tails(lane, cols):
+def pack_pair(low, high):
+    return jnp.where(lane_of(low.shape) < HALF, low, turned(high, HALF))
+
+
+def pack_tails(cols):
     out = jnp.zeros_like(cols[0])
+    lane = lane_of(out.shape)
     for i, col in enumerate(cols):
         out = jnp.where(lane // PIECE == i, turned(col, PIECE * i - HALF), out)
     return out
@@ -42,7 +44,7 @@
     xn, xt, base, quot, obs3, bt, pn, pb, rn, rb, en, eb, nu, xb, x3, acc, h3, score,
     qs, rq, st, red1, sum1, red2,
     bar_n_s, bar_n_r, bar_b_s, bar_b_r, edge_s, edge_n_r, edge_b_r, ret_s, ret_r,
-    r1_s, r1_r, r2_s, r2_r,
+    r1_s, r1_r, r2_s, r2_r, w1p, w2p, w1s, w2s,
 ):
     t = lax.axis_index("traj")
     b = lax.axis_index("lon")
@@ -109,11 +111,23 @@
             copies[i - 1].wait()
             tot = tot + red2[step, i]
         moment = jnp.sum(tot, axis=0, keepdims=True) / count
-        return jnp.broadcast_to(1.0 / jnp.sqrt(moment + 1e-06), (rows, LANES))
+        return 1.0 / jnp.sqrt(moment + 1e-06)
 
     part = squares(xt, 0, cols * rows)
     pl.semaphore_wait(barrier, partners)
     scale = reduced(0, part, True)
+
+    def tiled(value):
+        return value.reshape(-1, rows, LANES)
+
+    def flat(value):
+        return value.reshape(-1, LANES)
+
+    def pack_main(get, put):
+        step = cw // 8
+        for i in range(4):
+            put(i * step, pack_pair(get(i * step, step), get(cw // 2 + i * step, step)))
+        put(cw // 2, pack_tails([get(step * i, step) for i in range(8)]))
 
     def pack_all(get, dest):
         zero = jnp.zeros((3, rows, LANES), BF16)
@@ -121,23 +135,13 @@
         dest[nt, tiles - 3 :] = zero
 
         def sub(k, carry):
-            def pair(j, c):
-                dest[k + 1, 3 + j] = pack_pair(lane, get(k * cw + j), get(k * cw + j + cw // 2)).astype(BF16)
-                return c
-
-            lax.fori_loop(0, cw // 2, pair, 0, unroll=2)
-
-            def tail(j, c):
-                dest[k + 1, 3 + cw // 2 + j] = pack_tails(
-                    lane, [get(k * cw + j + cw // 8 * i) for i in range(8)]).astype(BF16)
-                return c
-
-            lax.fori_loop(0, cw // 8, tail, 0)
+            def put(j, v):
+                dest[k + 1, pl.ds(3 + j, v.shape[0] // rows)] = tiled(v.astype(BF16))
+
+            pack_main(lambda c, n: get(k * cw + c, n), put)
             for first, slot, at in ((k * cw, k, tiles - 3), (k * cw + cw - halo, k + 2, 0)):
-                four = [get(first + i) for i in range(4)]
-                dest[slot, at] = pack_pair(lane, four[0], four[2]).astype(BF16)
-                dest[slot, at + 1] = pack_pair(lane, four[1], four[3]).astype(BF16)
-                dest[slot, at + 2] = pack_tails(lane, four).astype(BF16)
+                dest[slot, at : at + 2] = tiled(pack_pair(get(first, 2), get(first + 2, 2)).astype(BF16))
+                dest[slot, at + 2] = pack_tails([get(first + i, 1) for i in range(4)]).astype(BF16)
             return carry
 
         lax.fori_loop(0, nt, sub, 0)
@@ -184,33 +188,30 @@
         def _():
             edges(tiles - 3, -1)
 
+    def unpack_main(tile, put):
+        step = cw // 8
+        tail = tile(cw // 2, step)
+        for i in range(8):
+            a = turned(tile((i % 4) * step, step), HALF * (i // 4))
+            put(i * step, jnp.where(lane_of(a.shape) < HALF, a, turned(tail, HALF - PIECE * i)))
+
     def unpack_all(src, put):
         def state(s, carry):
-            def tile(j):
-                return src[s, j].astype(F32)
+            def tile(j, n):
+                return flat(src[s, pl.ds(j, n)].astype(F32))
 
             for at, first in ((0, 0), (tiles - 3, cw + halo)):
-                pairs = [tile(at), tile(at + 1)]
-                tail = tile(at + 2)
+                pairs = tile(at, 2)
+                tail = tile(at + 2, 1)
                 for i in range(4):
-                    a = turned(pairs[i % 2], HALF * (i // 2))
+                    a = turned(pairs[(i % 2) * rows : (i % 2 + 1) * rows], HALF * (i // 2))
                     put(s, first + i, jnp.where(lane < HALF, a, turned(tail, HALF - PIECE * i)))
-            unpack_main(lambda j: tile(3 + j), lambda c, v: put(s, c + halo, v))
+            unpack_main(lambda j, n: tile(3 + j, n), lambda c, v: put(s, c + halo, v))
             return carry
 
         lax.fori_loop(0, nt, state, 0)
 
-    def unpack_main(tile, put):
-        for i in range(8):
-            def one(j, c, i=i):
-                at = i * (cw // 8) + j
-                a = turned(tile(at % (cw // 2) if isinstance(at, int) else at - (i // 4) * (cw // 2)), HALF * (i // 4))
-                put(at, jnp.where(lane < HALF, a, turned(tile(cw // 2 + j), HALF - PIECE * i)))
-                return c
-
-            lax.fori_loop(0, cw // 8, one, 0, unroll=2)
-
-    pack_all(lambda c: xt[pl.ds(c * rows, rows), :] * scale, pn)
+    pack_all(lambda c, n: xt[pl.ds(c * rows, n * rows), :] * scale, pn)
     sent_n = send_all(pn, rn, en, bar_n_s, bar_n_r, edge_n_r, 0)
 
     vals = jnp.concatenate([val_ref[...], jnp.ones((8, val_ref.shape[1]), F32)], 0) if nvar % 8 == 0 else None
@@ -243,92 +244,112 @@
         return c
 
     lax.fori_loop(0, rows, observe, 0)
-    pack_all(lambda c: bt[pl.ds(c * rows, rows), :], pb)
+    pack_all(lambda c, n: bt[pl.ds(c * rows, n * rows), :], pb)
     sent_b = send_all(pb, rb, eb, bar_b_s, bar_b_r, edge_b_r, 1)
+
+    wide = 2 * LANES
+    deep = 3 * nvar
+    used = w1_ref.shape[1]
+    w1p[:, used // LANES * LANES :] = jnp.zeros((hid, w1p.shape[1] - used // LANES * LANES), BF16)
+    w1p[:, 0:used] = w1_ref[...]
+    w2p[deep // PIECE * PIECE :, :] = jnp.zeros((wide - deep // PIECE * PIECE, w2p.shape[1]), BF16)
+    w2p[0:deep, :] = w2_ref[...]
+    for a in range(3):
+        for k in range(3):
+            tap, to = 3 * a + k, 3 * k + a
+            at = tap * deep // LANES * LANES
+            v = w1p[:, at : at + 3 * LANES].astype(F32)
+            off = tap * deep - at
+            v = v if off == 0 else pltpu.roll(v, 3 * LANES - off, 1)
+            v = jnp.where(lane_of((hid, wide)) < deep, v[:, 0:wide], 0.0)
+            w1s[to * wide : (to + 1) * wide, :] = v.T.astype(BF16)
+            v = w2p[:, tap * hid : (tap + 1) * hid].astype(F32)
+            w2s[to * hid : (to + 1) * hid, :] = v.T.astype(BF16)
 
     nu[0] = jnp.zeros(nu.shape[1:], F32)
     nu[nt + 1] = jnp.zeros(nu.shape[1:], F32)
     receive(pn, rn, en, bar_n_s, bar_n_r, edge_n_r, 0)
 
     def put_n(s, c, v):
-        nu[s + 1, c] = v
+        nu[s + 1, pl.ds(c, v.shape[0] // rows)] = tiled(v)
 
     unpack_all(rn, put_n)
 
     def spread(dest, c, tile_list):
         n = len(tile_list)
+        many = tile_list[0].shape[0]
+        rown = lax.broadcasted_iota(jnp.int32, (many, LANES), 0) % rows
         for i, v in enumerate(tile_list):
-            up = jnp.where(row == 0, 0.0, pltpu.roll(v, 1, 0))
-            down = jnp.where(row == rows - 1, 0.0, pltpu.roll(v, rows - 1, 0))
+            up = jnp.where(rown == 0, 0.0, pltpu.roll(v, 1, 0))
+            down = jnp.where(rown == rows - 1, 0.0, pltpu.roll(v, many - 1, 0))
             for a, piece in enumerate((up, v, down)):
-                dest[c, :, a * n * LANES + i * LANES : a * n * LANES + (i + 1) * LANES] = piece.astype(BF16)
-
-    wide = 2 * LANES
+                dest[pl.ds(c, many // rows), :, a * n * LANES + i * LANES : a * n * LANES + (i + 1) * LANES] = tiled(
+                    piece.astype(BF16))
+
     two = 2 * nvar - LANES
 
     def network(width):
         score[...] = jnp.zeros(score.shape, F32)
 
         def state(s, carry):
-            def window(c, k):
-                before, here, after = nu[s, c], nu[s + 1, c], nu[s + 2, c]
+            def window(j, k):
+                c = j * GROUP
+                before, here, after = [flat(nu[s + i, pl.ds(c, GROUP)]) for i in range(3)]
+                lane = lane_of(here.shape)
                 moved = turned(here, nvar)
                 first = jnp.where(lane < nvar, before, moved)
                 last = jnp.where(lane < two, moved, jnp.where(lane < two + nvar, turned(after, two), 0.0))
                 spread(x3, c, [first, last])
                 return k
 
-            lax.fori_loop(0, width, window, 0, unroll=2)
+            lax.fori_loop(0, width // GROUP, window, 0, unroll=2)
             wid = width - 2
             lhs = jnp.concatenate(
                 [x3[i : i + wid].reshape(wid * rows, 3 * wide) for i in range(3)], 1)
-            acc[0 : wid * rows, :] = jnp.dot(lhs, w1_ref[...], preferred_element_type=F32)
-            bias = jnp.broadcast_to(b1_ref[...], (rows, hid))
-
-            def activate(c, k):
-                v = acc[pl.ds(c * rows, rows), :] + bias
+            acc[0 : wid * rows, :] = jnp.dot(lhs, w1s[...], preferred_element_type=F32)
+            bias = b1_ref[...]
+
+            def activate(j, k):
+                c = jnp.minimum(j * GROUP, wid - GROUP)
+                v = acc[pl.ds(c * rows, GROUP * rows), :] + bias
                 v = v / (1.0 + jnp.exp(-v))
                 v = v.astype(BF16).astype(F32)
                 spread(h3, c, [v[:, i * LANES : (i + 1) * LANES] for i in range(hid // LANES)])
                 return k
 
-            lax.fori_loop(0, wid, activate, 0, unroll=2)
+            lax.fori_loop(0, -(-wid // GROUP), activate, 0, unroll=2)
             wid = width - 4
             lhs = jnp.concatenate(
                 [h3[i : i + wid].reshape(wid * rows, 3 * hid) for i in range(3)], 1)
-            acc[0 : wid * rows, :] = jnp.dot(lhs, w2_ref[...], preferred_element_type=F32)
-
-            def share(c, k):
-                c0 = acc[pl.ds(c * rows, rows), 0:LANES]
-                c1 = acc[pl.ds(c * rows, rows), LANES : 2 * LANES]
+            acc[0 : wid * rows, :] = jnp.dot(lhs, w2s[...], preferred_element_type=F32)
+
+            def share(j, k):
+                c = j * GROUP
+                c0 = acc[pl.ds(c * rows, GROUP * rows), 0:LANES]
+                c1 = acc[pl.ds(c * rows, GROUP * rows), LANES : 2 * LANES]
+                lane = lane_of(c0.shape)
                 mid_part = jnp.where(lane < LANES - nvar, turned(c0, -nvar), turned(c1, -nvar))
-                score[s, c] += c0
-                score[s + 1, c] += mid_part
-                score[s + 2, c] += turned(c1, -two)
+                at = pl.ds(c, GROUP)
+                olds = [score[s + i, at] for i in range(3)]
+                news = [old + tiled(v) for old, v in zip(olds, (c0, mid_part, turned(c1, -two)))]
+                for i in range(3):
+                    score[s + i, at] = news[i]
                 return k
 
-            lax.fori_loop(0, wid, share, 0, unroll=2)
+            lax.fori_loop(0, wid // GROUP, share, 0)
             return carry
 
         lax.fori_loop(0, nt, state, 0)
 
     def give_back(step, off):
         def state(s, carry):
-            def get(c):
-                return score[s + 1, c + off]
-
-            def pair(j, c):
-                qs[step, s, j] = pack_pair(lane, get(j), get(j + cw // 2)).astype(BF16)
-                return c
-
-            lax.fori_loop(0, cw // 2, pair, 0, unroll=2)
-
-            def tail(j, c):
-                qs[step, s, cw // 2 + j] = pack_tails(
-                    lane, [get(j + cw // 8 * i) for i in range(8)]).astype(BF16)
-                return c
-
-            lax.fori_loop(0, cw // 8, tail, 0)
+            def get(c, n):
+                return flat(score[s + 1, pl.ds(c + off, n)])
+
+            def put(j, v):
+                qs[step, s, pl.ds(j, v.shape[0] // rows)] = tiled(v.astype(BF16))
+
+            pack_main(get, put)
             return carry
 
         lax.fori_loop(0, nt, state, 0)
@@ -352,9 +373,9 @@
 
         def band(k, carry):
             def put(c, v):
-                st[pl.ds((k * cw + c) * rows, rows), :] = v
-
-            unpack_main(lambda j: rq[step, k, j].astype(F32), put)
+                st[pl.ds((k * cw + c) * rows, v.shape[0]), :] = v
+
+            unpack_main(lambda j, n: flat(rq[step, k, pl.ds(j, n)].astype(F32)), put)
             return carry
 
         lax.fori_loop(0, nt, band, 0)
@@ -365,17 +386,17 @@
     receive(pb, rb, eb, bar_b_s, bar_b_r, edge_b_r, 1)
 
     def put_x(s, c, v):
-        xb[s, c] = v
+        xb[s, pl.ds(c, v.shape[0] // rows)] = tiled(v)
 
     unpack_all(rb, put_x)
 
     def advance(s, total):
-        def one(c, k):
-            v = xb[s, c + 2] + 0.5 * score[s + 1, c]
-            nu[s + 1, c] = v
+        def one(j, k):
+            at = pl.ds(j * GROUP, GROUP)
+            nu[s + 1, at] = xb[s, pl.ds(j * GROUP + 2, GROUP)] + 0.5 * score[s + 1, at]
             return k
 
-        lax.fori_loop(0, ext - 4, one, 0, unroll=2)
+        lax.fori_loop(0, (ext - 4) // GROUP, one, 0)
 
         def sq(c, k):
             v = nu[s + 1, c + 2]
@@ -390,11 +411,12 @@
     scale = reduced(1, part, False)
 
     def rescale(s, carry):
-        def one(c, k):
-            nu[s + 1, c] = (nu[s + 1, c] * scale).astype(BF16).astype(F32)
+        def one(j, k):
+            at = pl.ds(j * GROUP, GROUP)
+            nu[s + 1, at] = (nu[s + 1, at] * scale).astype(BF16).astype(F32)
             return k
 
-        return lax.fori_loop(0, ext - 4, one, carry, unroll=2)
+        return lax.fori_loop(0, (ext - 4) // GROUP, one, carry)
 
     lax.fori_loop(0, nt, rescale, 0)
     network(ext - 4)
@@ -431,16 +453,13 @@
     lon_total = cols * nl
     loc = obs_index // lon_total * cols + obs_index % lon_total - band * cols
     wide = 2 * LANES
-    w1 = first_weight.reshape(hid, 3, 3, 3 * nvar)
-    w1 = jnp.pad(w1, ((0, 0), (0, 0), (0, 0), (0, wide - 3 * nvar)))
-    w1 = w1.transpose(2, 1, 3, 0).reshape(9 * wide, hid)
-    w2 = jnp.pad(second_weight, ((0, wide - 3 * nvar), (0, 0))).reshape(wide, 3, 3, hid)
-    w2 = w2.transpose(2, 1, 3, 0).reshape(9 * hid, wide)
+    span = (9 * 3 * nvar // LANES + 3) * LANES
     cw = cols // nt
     ext = cw + 4 * STEPS
     mt = 5 * cw // 8
     tiles = mt + 6
     nobs = obs_values.shape[2]
+    wide = 2 * LANES
     dma = pltpu.SemaphoreType.DMA
     vm = pltpu.VMEM
     big = LANES * rows
@@ -459,6 +478,7 @@
         dma((nt,)), dma((nt,)), dma((nt,)), dma((nt,)), dma((2, 2)), dma((nt,)), dma((nt,)),
         dma((STEPS, nt)), dma((STEPS, nt)),
         dma((STEPS, nt)), dma((STEPS, nt)), dma((STEPS, nl)), dma((STEPS, nl)),
+        vm((hid, span), BF16), vm((wide, 9 * hid), BF16), vm((9 * wide, hid), BF16), vm((9 * hid, wide), BF16),
     ]
     out = pl.pallas_call(
         functools.partial(kernel, nt, nl, nvar, rows, cols, hid),
@@ -468,7 +488,7 @@
         scratch_shapes=scratch,
         compiler_params=pltpu.CompilerParams(
             collective_id=0, has_side_effects=True, vmem_limit_bytes=60 << 20),
-    )(states.reshape(nvar * rows, cols), loc, obs_values[0], w1, first_bias.reshape(1, hid), w2)
+    )(states.reshape(nvar * rows, cols), loc, obs_values[0], first_weight, first_bias.reshape(1, hid), second_weight)
     return out.reshape(1, nvar, rows, cols)
 
 

time: 135 us -> 102 us (0.76)
  Pallas kernels: 127 us -> 94.6 us
  local copies, waits for them, and re-layouts: 7.45 us -> 5.82 us
    pallas_call x1, Pallas kernels: 127 us -> 94.6 us  [body(): pl.pallas_call(functools.partial(kernel, nt, nl, nvar, rows, cols, hid),...]
    unnamed x9 -> x3, local copies, waits for them, and re-layouts: 4.67 us -> 5.82 us
where the time goes in v1:
time: 102 us
  Pallas kernels  94.6 us (93%)
  local copies, waits for them, and re-layouts  5.82 us (6%)
  other arithmetic  1.27 us (1%)
    pallas_call x1, Pallas kernels, body(): pl.pallas_call(functools.partial(kernel, nt, nl, nvar, rows, cols, hid),...  94.6 us
    unnamed x3, local copies, waits for them, and re-layouts  5.82 us

profile of v1, /device:TPU:0, one launch (start us, length us, event | category | flops | bytes accessed | tf_op | source)
XLA Modules:
  0.0 101.7 jit_solution(14042792009839157140)
XLA Ops:
  0.0 1.3 %fusion.1.loc_ref = s32[1,256]{1,0:T(1,128)} fusion(s32[1,256]{1,0:T(1,128)} %param.7, s32[]{:T(128)S(6)} %mul.11), kind=kLoop, calls=%fused_computation.7 | loop fusion | flops 5632 | bytes 2052 | tf_op jit(solution)/shard_map/sub | solution.py:454
  1.3 1.5 %copy.10 = f32[1,78,256]{2,1,0:T(8,128)} copy(f32[1,78,256]{2,0,1:T(1,128)} %param.8) | data formatting | bytes 159744
  2.8 2.3 %copy.7.w1_ref = bf16[256,2106]{1,0:T(8,128)(2,1)} copy(bf16[256,2106]{0,1:T(8,128)(2,1)} %param.9) | data formatting | bytes 2156544 | tf_op args[3]
  5.1 94.6 %shard_map.64 = f32[1248,128]{1,0:T(8,128)} custom-call(f32[1248,128]{1,0:T(8,128)} %bitcast.7, s32[1,256]{1,0:T(1,128)} %fusion.1.loc_ref, f32[78,256]{1,0:T(8,128)} %bitcast.8, bf16[256,2106]{1,0:T(8,128)(2,1)} %copy.7.w1_ref, f32[1,256]{1,0:T(1,128)} %bitcast.9, bf16[234,2304]{1,0:T(8,128)(2,1)} %w2_ref.1), custom_call_target="tpu_custom_call" | custom-call | tf_op jit(solution)/shard_map/pallas_call | solution.py:483
  99.7 2.0 %copy.12 = f32[1,78,16,128]{3,2,1,0:T(8,128)} copy(f32[1,78,16,128]{3,2,1,0:T(8,128)} %bitcast.6) | data formatting | bytes 1277952

commit v2 on v1

v2 whole, which is shorter than its diff:
```python
import functools

import jax
import jax.numpy as jnp
from jax import lax
from jax.experimental import pallas as pl
from jax.experimental.pallas import tpu as pltpu
from jax.sharding import PartitionSpec as P

STEPS = 2
F32 = jnp.float32
BF16 = jnp.bfloat16
LANES = 128
HALF = 64
PIECE = 16
GROUP = 4
MESH = pl.DeviceIdType.MESH


def lane_of(shape):
    return lax.broadcasted_iota(jnp.int32, shape, len(shape) - 1)


def turned(value, by):
    by = by % LANES
    return value if by == 0 else pltpu.roll(value, by, len(value.shape) - 1)


def pack_pair(low, high):
    return jnp.where(lane_of(low.shape) < HALF, low, turned(high, HALF))


def pack_tails(cols):
    out = jnp.zeros_like(cols[0])
    lane = lane_of(out.shape)
    for i, col in enumerate(cols):
        out = jnp.where(lane // PIECE == i, turned(col, PIECE * i - HALF), out)
    return out


def kernel(
    nt, nl, nvar, rows, cols, hid,
    x_ref, loc_ref, val_ref, w1_ref, b1_ref, w2_ref, out_ref,
    xn, xt, base, quot, obs3, bt, pn, pb, rn, rb, en, eb, nu, xb, x3, acc, h3, score,
    qs, rq, st, red1, sum1, red2,
    bar_n_s, bar_n_r, bar_b_s, bar_b_r, edge_s, edge_n_r, edge_b_r, ret_s, ret_r,
    r1_s, r1_r, r2_s, r2_r, w2p, w1s, w2s,
):
    t = lax.axis_index("traj")
    b = lax.axis_index("lon")
    cw = cols // nt
    halo = 2 * STEPS
    ext = cw + 2 * halo
    mt = 5 * cw // 8
    tiles = mt + 6
    count = nt * rows * cols * nl
    lane = lane_of((rows, LANES))
    row = lax.broadcasted_iota(jnp.int32, (rows, LANES), 0)

    def dev(tt, bb):
        return {"traj": lax.rem(tt, nt), "lon": lax.rem(bb, nl)}

    upward = 2 * t < nt

    def nth(i):
        return jnp.where(upward, i, nt - 1 - i)

    own_place = nth(t)

    def other(j):
        return nth(j + jnp.where(j >= own_place, 1, 0))

    barrier = pltpu.get_barrier_semaphore()
    partners = 0
    for db in range(nl):
        for dt in range(nt):
            near = db in (0, 1, nl - 1)
            if (db or dt) and (near or dt == 0):
                pl.semaphore_signal(barrier, inc=1, device_id=dev(t + dt, b + db), device_id_type=MESH)
                partners += 1

    xn[0 : nvar * rows, :] = x_ref[...]
    xn[nvar * rows :, :] = jnp.zeros((LANES * rows - nvar * rows, LANES), F32)

    def flip(r, c):
        xt[pl.ds(r, cols, stride=rows), :] = xn[pl.ds(r, LANES, stride=rows), :].T
        return c

    lax.fori_loop(0, rows, flip, 0, unroll=4)

    def squares(ref, first, n):
        def one(i, c):
            v = ref[pl.ds(first + i * 32, 32), :]
            return c + v * v

        s = lax.fori_loop(0, n // 32, one, jnp.zeros((32, LANES), F32))
        return s[0:8] + s[8:16] + s[16:24] + s[24:32]

    def sum_over_traj(step, part):
        sum1[step, 0] = part
        copies = [
            pltpu.make_async_remote_copy(
                sum1.at[step, 0], red1.at[step, i], r1_s.at[step, i], r1_r.at[step, i],
                device_id=dev(t + i, b), device_id_type=MESH)
            for i in range(1, nt)]
        for cp in copies:
            cp.start()
        return copies

    def sum_over_lon(step, part, copies):
        tot = part
        for i, cp in enumerate(copies):
            cp.wait()
            tot = tot + red1[step, i + 1]
        sum1[step, 1] = tot
        copies = [
            pltpu.make_async_remote_copy(
                sum1.at[step, 1], red2.at[step, i], r2_s.at[step, i], r2_r.at[step, i],
                device_id=dev(t, b + i), device_id_type=MESH)
            for i in range(1, nl)]
        for cp in copies:
            cp.start()
        return tot, copies

    def scale_of(step, tot, copies):
        for i, cp in enumerate(copies):
            cp.wait()
            tot = tot + red2[step, i + 1]
        moment = jnp.sum(tot, axis=0, keepdims=True) / count
        return 1.0 / jnp.sqrt(moment + 1e-06)

    part = squares(xt, 0, cols * rows)
    pl.semaphore_wait(barrier, partners)
    moving = sum_over_traj(0, part)

    obs3[0] = jnp.ones(obs3.shape[1:], F32)
    obs3[0, 0:nvar] = val_ref[:, 0, :]
    full = obs3[0]
    high = full.astype(BF16)
    rest = full - high.astype(F32)
    mid = rest.astype(BF16)
    low = (rest - mid.astype(F32)).astype(BF16)
    three = jnp.concatenate([high, mid, low], 0)
    loc = loc_ref[...]

    def observe(r, c):
        cell = lax.broadcasted_iota(jnp.int32, (cols, loc.shape[1]), 0) + (r * cols * nl + b * cols)
        hot = jnp.where(cell == loc, 1.0, 0.0).astype(BF16)
        o = lax.dot_general(three, hot, (((1,), (1,)), ((), ())), preferred_element_type=F32)
        o = o[0:LANES] + o[LANES : 2 * LANES] + o[2 * LANES :]
        seen = o[nvar : nvar + 1, :] > 0.5
        x = xn[pl.ds(r, LANES, stride=rows), :]
        g = jnp.where(seen, 0.5 * (o - x), 0.0)
        base[pl.ds(r, LANES, stride=rows), :] = jnp.where(seen, 0.5 * (x + g + o), x)
        quot[pl.ds(r, 1), :] = jnp.where(seen, 0.25, 0.5)
        bt[pl.ds(r, cols, stride=rows), :] = (x + g).T
        return c

    lax.fori_loop(0, rows, observe, 0, unroll=2)
    part, moving = sum_over_lon(0, part, moving)

    wide = 2 * LANES
    deep = 3 * nvar
    w2p[deep // PIECE * PIECE :, :] = jnp.zeros((wide - deep // PIECE * PIECE, w2p.shape[1]), BF16)
    w2p[0:deep, :] = w2_ref[...]
    for a in range(3):
        for k in range(3):
            tap, to = 3 * a + k, 3 * k + a
            w1s[(to + 1) * wide - 2 * PIECE : (to + 1) * wide, :] = jnp.zeros((2 * PIECE, hid), BF16)
            w1s[to * wide : to * wide + deep, :] = w1_ref[tap * deep : (tap + 1) * deep, :]
            v = w2p[:, tap * hid : (tap + 1) * hid].astype(F32)
            w2s[to * hid : (to + 1) * hid, :] = v.T.astype(BF16)

    scale = scale_of(0, part, moving)

    def tiled(value):
        return value.reshape(-1, rows, LANES)

    def flat(value):
        return value.reshape(-1, LANES)

    def pack_main(get, put):
        step = cw // 8
        for i in range(4):
            put(i * step, pack_pair(get(i * step, step), get(cw // 2 + i * step, step)))
        put(cw // 2, pack_tails([get(step * i, step) for i in range(8)]))

    def pack_all(get, dest):
        zero = jnp.zeros((3, rows, LANES), BF16)
        dest[1, 0:3] = zero
        dest[nt, tiles - 3 :] = zero

        def sub(k, carry):
            def put(j, v):
                dest[k + 1, pl.ds(3 + j, v.shape[0] // rows)] = tiled(v.astype(BF16))

            pack_main(lambda c, n: get(k * cw + c, n), put)
            for first, slot, at in ((k * cw, k, tiles - 3), (k * cw + cw - halo, k + 2, 0)):
                dest[slot, at : at + 2] = tiled(pack_pair(get(first, 2), get(first + 2, 2)).astype(BF16))
                dest[slot, at + 2] = pack_tails([get(first + i, 1) for i in range(4)]).astype(BF16)
            return carry

        lax.fori_loop(0, nt, sub, 0)

    def send_all(src, dst, edge, s_sem, r_sem, e_sem, f):
        right = pltpu.make_async_remote_copy(
            src.at[nt + 1, 0:3], edge.at[t], edge_s.at[f, 0], e_sem.at[t],
            device_id=dev(0, b + 1), device_id_type=MESH)
        left = pltpu.make_async_remote_copy(
            src.at[0, tiles - 3 : tiles], edge.at[t], edge_s.at[f, 1], e_sem.at[t],
            device_id=dev(nt - 1, b + nl - 1), device_id_type=MESH)
        right.start()
        left.start()
        copies = [right, left]
        for j in range(nt - 1):
            k = other(j)
            cp = pltpu.make_async_remote_copy(
                src.at[k + 1], dst.at[t], s_sem.at[j], r_sem.at[t],
                device_id=dev(k, b), device_id_type=MESH)
            cp.start()
            copies.append(cp)
        dst[t] = src[t + 1]
        return copies

    def receive(s, src, dst, edge, s_sem, r_sem, e_sem, f):
        @pl.when(s != t)
        def _():
            pltpu.make_async_remote_copy(
                src.at[s + 1], dst.at[s], s_sem.at[0], r_sem.at[s],
                device_id=dev(s, b), device_id_type=MESH).wait_recv()

        def edges(at):
            pltpu.make_async_remote_copy(
                src.at[0, 0:3], edge.at[s], edge_s.at[f, 0], e_sem.at[s],
                device_id=dev(0, b + 1), device_id_type=MESH).wait_recv()
            dst[s, at : at + 3] = edge[s]

        @pl.when(t == 0)
        def _():
            edges(0)

        @pl.when(t == nt - 1)
        def _():
            edges(tiles - 3)

    def unpack_main(tile, put):
        step = cw // 8
        tail = tile(cw // 2, step)
        for i in range(8):
            a = turned(tile((i % 4) * step, step), HALF * (i // 4))
            put(i * step, jnp.where(lane_of(a.shape) < HALF, a, turned(tail, HALF - PIECE * i)))

    def unpack_state(s, src, put):
        def tile(j, n):
            return flat(src[s, pl.ds(j, n)].astype(F32))

        for at, first in ((0, 0), (tiles - 3, cw + halo)):
            pairs = tile(at, 2)
            tail = tile(at + 2, 1)
            for i in range(4):
                a = turned(pairs[(i % 2) * rows : (i % 2 + 1) * rows], HALF * (i // 2))
                put(s, first + i, jnp.where(lane < HALF, a, turned(tail, HALF - PIECE * i)))
        unpack_main(lambda j, n: tile(3 + j, n), lambda c, v: put(s, c + halo, v))

    pack_all(lambda c, n: xt[pl.ds(c * rows, n * rows), :] * scale, pn)
    sent_n = send_all(pn, rn, en, bar_n_s, bar_n_r, edge_n_r, 0)

    pack_all(lambda c, n: bt[pl.ds(c * rows, n * rows), :], pb)
    sent_b = send_all(pb, rb, eb, bar_b_s, bar_b_r, edge_b_r, 1)

    nu[0] = jnp.zeros(nu.shape[1:], F32)
    nu[nt + 1] = jnp.zeros(nu.shape[1:], F32)

    def put_n(s, c, v):
        nu[s + 1, pl.ds(c, v.shape[0] // rows)] = tiled(v)

    def arrive(s):
        receive(s, pn, rn, en, bar_n_s, bar_n_r, edge_n_r, 0)
        unpack_state(s, rn, put_n)

    def spread(dest, c, tile_list):
        n = len(tile_list)
        many = tile_list[0].shape[0]
        rown = lax.broadcasted_iota(jnp.int32, (many, LANES), 0) % rows
        for i, v in enumerate(tile_list):
            up = jnp.where(rown == 0, 0.0, pltpu.roll(v, 1, 0))
            down = jnp.where(rown == rows - 1, 0.0, pltpu.roll(v, many - 1, 0))
            for a, piece in enumerate((up, v, down)):
                dest[pl.ds(c, many // rows), :, a * n * LANES + i * LANES : a * n * LANES + (i + 1) * LANES] = tiled(
                    piece.astype(BF16))

    two = 2 * nvar - LANES

    def give_back(s, step, off):
        def get(c, n):
            return flat(score[s + 1, pl.ds(c + off, n)])

        def put(j, v):
            qs[step, s, pl.ds(j, v.shape[0] // rows)] = tiled(v.astype(BF16))

        pack_main(get, put)

        @pl.when(s != t)
        def _():
            pltpu.make_async_remote_copy(
                qs.at[step, s], rq.at[step, t], ret_s.at[step, s], ret_r.at[step, t],
                device_id=dev(s, b), device_id_type=MESH).start()

        @pl.when(s == t)
        def _():
            rq[step, t] = qs[step, s]

    def network(width, step, off):
        score[...] = jnp.zeros(score.shape, F32)

        def state(i, carry):
            s = nth(i) if step == 0 else nth(nt - 1 - i)
            if step == 0:
                @pl.when(i < nt - 1)
                def _():
                    arrive(nth(i + 1))

            def window(j, k):
                c = j * GROUP
                before, here, after = [flat(nu[s + i, pl.ds(c, GROUP)]) for i in range(3)]
                lane = lane_of(here.shape)
                moved = turned(here, nvar)
                first = jnp.where(lane < nvar, before, moved)
                last = jnp.where(lane < two, moved, jnp.where(lane < two + nvar, turned(after, two), 0.0))
                spread(x3, c, [first, last])
                return k

            lax.fori_loop(0, width // GROUP, window, 0, unroll=2)
            wid = width - 2
            lhs = jnp.concatenate(
                [x3[i : i + wid].reshape(wid * rows, 3 * wide) for i in range(3)], 1)
            acc[0 : wid * rows, :] = jnp.dot(lhs, w1s[...], preferred_element_type=F32)
            bias = b1_ref[...]

            def activate(j, k):
                c = jnp.minimum(j * GROUP, wid - GROUP)
                v = acc[pl.ds(c * rows, GROUP * rows), :] + bias
                v = 0.5 * v
                v = v + v * jnp.tanh(v)
                v = v.astype(BF16).astype(F32)
                spread(h3, c, [v[:, i * LANES : (i + 1) * LANES] for i in range(hid // LANES)])
                return k

            lax.fori_loop(0, -(-wid // GROUP), activate, 0, unroll=2)
            wid = width - 4
            lhs = jnp.concatenate(
                [h3[i : i + wid].reshape(wid * rows, 3 * hid) for i in range(3)], 1)
            acc[0 : wid * rows, :] = jnp.dot(lhs, w2s[...], preferred_element_type=F32)

            def share(j, k):
                c = j * GROUP
                c0 = acc[pl.ds(c * rows, GROUP * rows), 0:LANES]
                c1 = acc[pl.ds(c * rows, GROUP * rows), LANES : 2 * LANES]
                lane = lane_of(c0.shape)
                mid_part = jnp.where(lane < LANES - nvar, turned(c0, -nvar), turned(c1, -nvar))
                at = pl.ds(c, GROUP)
                olds = [score[s + i, at] for i in range(3)]
                news = [old + tiled(v) for old, v in zip(olds, (c0, mid_part, turned(c1, -two)))]
                for i in range(3):
                    score[s + i, at] = news[i]
                return k

            lax.fori_loop(0, wid // GROUP, share, 0)

            @pl.when(i > 0)
            def _():
                give_back(nth(i - 1) if step == 0 else nth(nt - i), step, off)

            return carry

        lax.fori_loop(0, nt, state, 0)
        give_back(nth(nt - 1) if step == 0 else nth(0), step, off)

    def take_back(step):
        for i in range(1, nt):
            k = lax.rem(t + i, nt)
            pltpu.make_async_remote_copy(
                qs.at[step, k], rq.at[step, k], ret_s.at[step, k], ret_r.at[step, k],
                device_id=dev(k, b), device_id_type=MESH).wait_recv()

        def band(k, carry):
            def put(c, v):
                st[pl.ds((k * cw + c) * rows, v.shape[0]), :] = v

            unpack_main(lambda j, n: flat(rq[step, k, pl.ds(j, n)].astype(F32)), put)
            return carry

        lax.fori_loop(0, nt, band, 0)

    arrive(nth(0))
    network(ext, 0, 2)


    def put_x(s, c, v):
        xb[s, pl.ds(c, v.shape[0] // rows)] = tiled(v)

    def arrive_base(i, carry):
        s = nth(i)
        receive(s, pb, rb, eb, bar_b_s, bar_b_r, edge_b_r, 1)
        unpack_state(s, rb, put_x)
        return carry

    lax.fori_loop(0, nt, arrive_base, 0)

    def advance(s, total):
        def one(j, k):
            at = pl.ds(j * GROUP, GROUP)
            nu[s + 1, at] = xb[s, pl.ds(j * GROUP + 2, GROUP)] + 0.5 * score[s + 1, at]
            return k

        lax.fori_loop(0, (ext - 4) // GROUP, one, 0)

        def sq(c, k):
            v = nu[s + 1, c + 2]
            return k + v * v

        return lax.fori_loop(0, cw, sq, total, unroll=2)

    total = lax.fori_loop(0, nt, advance, jnp.zeros((rows, LANES), F32))
    part = total[0:8]
    for i in range(1, rows // 8):
        part = part + total[8 * i : 8 * i + 8]
    moving = sum_over_traj(1, part)
    part, moving = sum_over_lon(1, part, moving)
    scale = scale_of(1, part, moving)

    def rescale(s, carry):
        def one(j, k):
            at = pl.ds(j * GROUP, GROUP)
            nu[s + 1, at] = (nu[s + 1, at] * scale).astype(BF16).astype(F32)
            return k

        return lax.fori_loop(0, (ext - 4) // GROUP, one, carry)

    lax.fori_loop(0, nt, rescale, 0)
    network(ext - 4, 1, 0)

    take_back(0)

    def add_first(r, c):
        v = st[pl.ds(r, cols, stride=rows), :].T
        at = pl.ds(r, LANES, stride=rows)
        base[at, :] = base[at, :] + quot[pl.ds(r, 1), :] * v
        return c

    lax.fori_loop(0, rows, add_first, 0)
    take_back(1)

    def add_second(r, c):
        v = st[pl.ds(r, cols, stride=rows), :].T
        at = pl.ds(r, LANES, stride=rows)
        base[at, :] = base[at, :] + 0.5 * v
        return c

    lax.fori_loop(0, rows, add_second, 0)
    out_ref[...] = base[0 : nvar * rows, :]
    for cp in sent_n + sent_b:
        cp.wait_send()
    for step in range(STEPS):
        for i in range(1, nt):
            k = lax.rem(t + i, nt)
            pltpu.make_async_remote_copy(
                qs.at[step, k], rq.at[step, t], ret_s.at[step, k], ret_r.at[step, t],
                device_id=dev(k, b), device_id_type=MESH).wait_send()


def body(states, obs_index, obs_values, first_weight, first_bias, second_weight):
    nt, nl = lax.axis_size("traj"), lax.axis_size("lon")
    _, nvar, rows, cols = states.shape
    hid = first_bias.shape[0]
    wide = 2 * LANES
    cw = cols // nt
    ext = cw + 4 * STEPS
    mt = 5 * cw // 8
    tiles = mt + 6
    nobs = obs_values.shape[2]
    dma = pltpu.SemaphoreType.DMA
    vm = pltpu.VMEM
    big = LANES * rows
    scratch = [
        vm((big, LANES), F32), vm((cols * rows, LANES), F32), vm((big, LANES), F32), vm((rows, LANES), F32),
        vm((1, LANES, nobs), F32), vm((cols * rows, LANES), F32),
        vm((nt + 2, tiles, rows, LANES), BF16), vm((nt + 2, tiles, rows, LANES), BF16),
        vm((nt, tiles, rows, LANES), BF16), vm((nt, tiles, rows, LANES), BF16),
        vm((nt, 3, rows, LANES), BF16), vm((nt, 3, rows, LANES), BF16),
        vm((nt + 2, ext, rows, LANES), F32), vm((nt, ext, rows, LANES), F32),
        vm((ext, rows, 3 * wide), BF16), vm((ext * rows, wide), F32), vm((ext, rows, 3 * hid), BF16),
        vm((nt + 2, ext - 4, rows, LANES), F32),
        vm((STEPS, nt, mt, rows, LANES), BF16), vm((STEPS, nt, mt, rows, LANES), BF16),
        vm((cols * rows, LANES), F32),
        vm((STEPS, nt, 8, LANES), F32), vm((STEPS, 2, 8, LANES), F32), vm((STEPS, nl, 8, LANES), F32),
        dma((nt,)), dma((nt,)), dma((nt,)), dma((nt,)), dma((2, 2)), dma((nt,)), dma((nt,)),
        dma((STEPS, nt)), dma((STEPS, nt)),
        dma((STEPS, nt)), dma((STEPS, nt)), dma((STEPS, nl)), dma((STEPS, nl)),
        vm((wide, 9 * hid), BF16), vm((9 * wide, hid), BF16), vm((9 * hid, wide), BF16),
    ]
    out = pl.pallas_call(
        functools.partial(kernel, nt, nl, nvar, rows, cols, hid),
        out_shape=jax.ShapeDtypeStruct((nvar * rows, cols), F32),
        in_specs=[pl.BlockSpec(memory_space=vm)] * 6,
        out_specs=pl.BlockSpec(memory_space=vm),
        scratch_shapes=scratch,
        compiler_params=pltpu.CompilerParams(
            collective_id=0, has_side_effects=True, vmem_limit_bytes=60 << 20),
    )(states.reshape(nvar * rows, cols), obs_index, obs_values.reshape(nvar, 1, nobs), first_weight.T, first_bias.reshape(1, hid), second_weight)
    return out.reshape(1, nvar, rows, cols)


def solution(mesh):
    placed = (P("traj", None, None, "lon"), P("traj", "lon"), P("traj", None, "lon"), P(), P(), P())
    return jax.shard_map(
        body, mesh=mesh, in_specs=placed, out_specs=P("traj", None, None, "lon"), check_vma=False
    )
```

time: 102 us -> 80.7 us (0.79)
  Pallas kernels: 94.6 us -> 78.6 us
  local copies, waits for them, and re-layouts: 5.82 us -> 1.95 us
  other arithmetic: 1.27 us -> 0 us
    pallas_call x1, Pallas kernels: 94.6 us -> 78.6 us  [body(): pl.pallas_call(functools.partial(kernel, nt, nl, nvar, rows, cols, hid),...]
    unnamed x3 -> x1, local copies, waits for them, and re-layouts: 5.82 us -> 1.95 us
    sub x1 -> x0, other arithmetic: 1.27 us -> none  [body(): loc = obs_index // lon_total * cols + obs_index % lon_total - band * cols]
where the time goes in v2:
time: 80.7 us; the launch traced here: 80.5 us
  Pallas kernels  78.6 us (97%)
  local copies, waits for them, and re-layouts  1.95 us (2%)
    pallas_call x1, Pallas kernels, body(): pl.pallas_call(functools.partial(kernel, nt, nl, nvar, rows, cols, hid),...  78.6 us
    unnamed x1, local copies, waits for them, and re-layouts  1.95 us

profile of v2, /device:TPU:0, one launch (start us, length us, event | category | flops | bytes accessed | tf_op | source)
XLA Modules:
  0.0 80.5 jit_solution(17654355381713127435)
XLA Ops:
  0.0 78.6 %shard_map.64 = f32[1248,128]{1,0:T(8,128)} custom-call(f32[1248,128]{1,0:T(8,128)} %bitcast.7, s32[1,256]{1,0:T(1,128)} %loc_ref.1, f32[78,1,256]{2,1,0:T(1,128)} %bitcast.8, bf16[2106,256]{1,0:T(8,128)(2,1)} %bitcast.6, f32[1,256]{1,0:T(1,128)} %bitcast.9, bf16[234,2304]{1,0:T(8,128)(2,1)} %w2_ref.1), custom_call_target="tpu_custom_call" | custom-call | tf_op jit(solution)/shard_map/pallas_call | solution.py:502
  78.6 2.0 %copy.8 = f32[1,78,16,128]{3,2,1,0:T(8,128)} copy(f32[1,78,16,128]{3,2,1,0:T(8,128)} %bitcast.5) | data formatting | bytes 1277952

commit v3 on v2

--- a/solution.py
+++ b/solution.py
@@ -41,7 +41,7 @@
 def kernel(
     nt, nl, nvar, rows, cols, hid,
     x_ref, loc_ref, val_ref, w1_ref, b1_ref, w2_ref, out_ref,
-    xn, xt, base, quot, obs3, bt, pn, pb, rn, rb, en, eb, nu, xb, x3, acc, h3, score,
+    xn, xt, base, kept, obs3, bt, pn, pb, rn, rb, en, eb, nu, xb, x3, acc, h3, score,
     qs, rq, st, red1, sum1, red2,
     bar_n_s, bar_n_r, bar_b_s, bar_b_r, edge_s, edge_n_r, edge_b_r, ret_s, ret_r,
     r1_s, r1_r, r2_s, r2_r, w2p, w1s, w2s,
@@ -152,7 +152,6 @@
         x = xn[pl.ds(r, LANES, stride=rows), :]
         g = jnp.where(seen, 0.5 * (o - x), 0.0)
         base[pl.ds(r, LANES, stride=rows), :] = jnp.where(seen, 0.5 * (x + g + o), x)
-        quot[pl.ds(r, 1), :] = jnp.where(seen, 0.25, 0.5)
         bt[pl.ds(r, cols, stride=rows), :] = (x + g).T
         return c
 
@@ -268,6 +267,8 @@
     pack_all(lambda c, n: bt[pl.ds(c * rows, n * rows), :], pb)
     sent_b = send_all(pb, rb, eb, bar_b_s, bar_b_r, edge_b_r, 1)
 
+    acc[0] = jnp.zeros(acc.shape[1:], F32)
+    acc[nt + 1] = jnp.zeros(acc.shape[1:], F32)
     nu[0] = jnp.zeros(nu.shape[1:], F32)
     nu[nt + 1] = jnp.zeros(nu.shape[1:], F32)
 
@@ -291,28 +292,39 @@
 
     two = 2 * nvar - LANES
 
-    def give_back(s, step, off):
+    def combine(s, wid):
+        def share(j, k):
+            at = pl.ds(j * GROUP * rows, GROUP * rows)
+            above = acc[s + 2, at, 0:LANES]
+            c0 = acc[s + 1, at, 0:LANES]
+            c1 = acc[s + 1, at, LANES : 2 * LANES]
+            below = acc[s, at, LANES : 2 * LANES]
+            here = turned(jnp.where(lane_of(c0.shape) >= nvar, c0, c1), -nvar)
+            score[s + 1, pl.ds(j * GROUP, GROUP)] = tiled(here + above + turned(below, -two))
+            return k
+
+        lax.fori_loop(0, wid // GROUP, share, 0, unroll=2 if wid // GROUP % 2 == 0 else 1)
+
+    def give_back(s):
         def get(c, n):
-            return flat(score[s + 1, pl.ds(c + off, n)])
+            return flat(0.5 * score[s + 1, pl.ds(c, n)] + kept[s, pl.ds(c + 2, n)])
 
         def put(j, v):
-            qs[step, s, pl.ds(j, v.shape[0] // rows)] = tiled(v.astype(BF16))
+            qs[s, pl.ds(j, v.shape[0] // rows)] = tiled(v.astype(BF16))
 
         pack_main(get, put)
 
         @pl.when(s != t)
         def _():
             pltpu.make_async_remote_copy(
-                qs.at[step, s], rq.at[step, t], ret_s.at[step, s], ret_r.at[step, t],
+                qs.at[s], rq.at[t], ret_s.at[s], ret_r.at[t],
                 device_id=dev(s, b), device_id_type=MESH).start()
 
         @pl.when(s == t)
         def _():
-            rq[step, t] = qs[step, s]
-
-    def network(width, step, off):
-        score[...] = jnp.zeros(score.shape, F32)
-
+            rq[t] = qs[s]
+
+    def network(width, step):
         def state(i, carry):
             s = nth(i) if step == 0 else nth(nt - 1 - i)
             if step == 0:
@@ -332,68 +344,57 @@
 
             lax.fori_loop(0, width // GROUP, window, 0, unroll=2)
             wid = width - 2
-            lhs = jnp.concatenate(
-                [x3[i : i + wid].reshape(wid * rows, 3 * wide) for i in range(3)], 1)
-            acc[0 : wid * rows, :] = jnp.dot(lhs, w1s[...], preferred_element_type=F32)
             bias = b1_ref[...]
-
-            def activate(j, k):
-                c = jnp.minimum(j * GROUP, wid - GROUP)
-                v = acc[pl.ds(c * rows, GROUP * rows), :] + bias
-                v = 0.5 * v
-                v = v + v * jnp.tanh(v)
-                v = v.astype(BF16).astype(F32)
-                spread(h3, c, [v[:, i * LANES : (i + 1) * LANES] for i in range(hid // LANES)])
-                return k
-
-            lax.fori_loop(0, -(-wid // GROUP), activate, 0, unroll=2)
+            chunk = wid // 2
+            for start in range(0, wid, chunk):
+                lhs = jnp.concatenate(
+                    [x3[start + k : start + k + chunk].reshape(chunk * rows, 3 * wide) for k in range(3)], 1)
+                whole = jnp.dot(lhs, w1s[...], preferred_element_type=F32)
+                for c in range(0, chunk, GROUP):
+                    n = min(GROUP, chunk - c)
+                    v = whole[c * rows : (c + n) * rows] + bias
+                    v = 0.5 * v
+                    v = v + v * jnp.tanh(v)
+                    v = v.astype(BF16).astype(F32)
+                    spread(h3, start + c, [v[:, m * LANES : (m + 1) * LANES] for m in range(hid // LANES)])
             wid = width - 4
             lhs = jnp.concatenate(
-                [h3[i : i + wid].reshape(wid * rows, 3 * hid) for i in range(3)], 1)
-            acc[0 : wid * rows, :] = jnp.dot(lhs, w2s[...], preferred_element_type=F32)
-
-            def share(j, k):
-                c = j * GROUP
-                c0 = acc[pl.ds(c * rows, GROUP * rows), 0:LANES]
-                c1 = acc[pl.ds(c * rows, GROUP * rows), LANES : 2 * LANES]
-                lane = lane_of(c0.shape)
-                mid_part = jnp.where(lane < LANES - nvar, turned(c0, -nvar), turned(c1, -nvar))
-                at = pl.ds(c, GROUP)
-                olds = [score[s + i, at] for i in range(3)]
-                news = [old + tiled(v) for old, v in zip(olds, (c0, mid_part, turned(c1, -two)))]
-                for i in range(3):
-                    score[s + i, at] = news[i]
-                return k
-
-            lax.fori_loop(0, wid // GROUP, share, 0)
+                [h3[k : k + wid].reshape(wid * rows, 3 * hid) for k in range(3)], 1)
+            acc[s + 1, 0 : wid * rows, :] = jnp.dot(lhs, w2s[...], preferred_element_type=F32)
 
             @pl.when(i > 0)
             def _():
-                give_back(nth(i - 1) if step == 0 else nth(nt - i), step, off)
+                done = nth(i - 1) if step == 0 else nth(nt - i)
+                combine(done, width - 4)
+                if step:
+                    give_back(done)
 
             return carry
 
         lax.fori_loop(0, nt, state, 0)
-        give_back(nth(nt - 1) if step == 0 else nth(0), step, off)
-
-    def take_back(step):
+        done = nth(nt - 1) if step == 0 else nth(0)
+        combine(done, width - 4)
+        if step:
+            give_back(done)
+
+    def take_back():
         for i in range(1, nt):
             k = lax.rem(t + i, nt)
             pltpu.make_async_remote_copy(
-                qs.at[step, k], rq.at[step, k], ret_s.at[step, k], ret_r.at[step, k],
+                qs.at[k], rq.at[k], ret_s.at[k], ret_r.at[k],
                 device_id=dev(k, b), device_id_type=MESH).wait_recv()
 
         def band(k, carry):
             def put(c, v):
                 st[pl.ds((k * cw + c) * rows, v.shape[0]), :] = v
 
-            unpack_main(lambda j, n: flat(rq[step, k, pl.ds(j, n)].astype(F32)), put)
+            unpack_main(lambda j, n: flat(rq[k, pl.ds(j, n)].astype(F32)), put)
             return carry
 
         lax.fori_loop(0, nt, band, 0)
 
     arrive(nth(0))
-    network(ext, 0, 2)
+    network(ext, 0)
 
 
     def put_x(s, c, v):
@@ -410,7 +411,10 @@
     def advance(s, total):
         def one(j, k):
             at = pl.ds(j * GROUP, GROUP)
-            nu[s + 1, at] = xb[s, pl.ds(j * GROUP + 2, GROUP)] + 0.5 * score[s + 1, at]
+            here = flat(xb[s, pl.ds(j * GROUP + 2, GROUP)])
+            change = flat(score[s + 1, at])
+            nu[s + 1, at] = tiled(here + 0.5 * change)
+            kept[s, at] = tiled((0.5 - 0.5 * here[:, nvar : nvar + 1]) * change)
             return k
 
         lax.fori_loop(0, (ext - 4) // GROUP, one, 0)
@@ -438,35 +442,25 @@
         return lax.fori_loop(0, (ext - 4) // GROUP, one, carry)
 
     lax.fori_loop(0, nt, rescale, 0)
-    network(ext - 4, 1, 0)
-
-    take_back(0)
-
-    def add_first(r, c):
-        v = st[pl.ds(r, cols, stride=rows), :].T
-        at = pl.ds(r, LANES, stride=rows)
-        base[at, :] = base[at, :] + quot[pl.ds(r, 1), :] * v
-        return c
-
-    lax.fori_loop(0, rows, add_first, 0)
-    take_back(1)
+    network(ext - 4, 1)
+
+    take_back()
 
     def add_second(r, c):
         v = st[pl.ds(r, cols, stride=rows), :].T
         at = pl.ds(r, LANES, stride=rows)
-        base[at, :] = base[at, :] + 0.5 * v
+        base[at, :] = base[at, :] + v
         return c
 
-    lax.fori_loop(0, rows, add_second, 0)
+    lax.fori_loop(0, rows, add_second, 0, unroll=4)
     out_ref[...] = base[0 : nvar * rows, :]
     for cp in sent_n + sent_b:
         cp.wait_send()
-    for step in range(STEPS):
-        for i in range(1, nt):
-            k = lax.rem(t + i, nt)
-            pltpu.make_async_remote_copy(
-                qs.at[step, k], rq.at[step, t], ret_s.at[step, k], ret_r.at[step, t],
-                device_id=dev(k, b), device_id_type=MESH).wait_send()
+    for i in range(1, nt):
+        k = lax.rem(t + i, nt)
+        pltpu.make_async_remote_copy(
+            qs.at[k], rq.at[t], ret_s.at[k], ret_r.at[t],
+            device_id=dev(k, b), device_id_type=MESH).wait_send()
 
 
 def body(states, obs_index, obs_values, first_weight, first_bias, second_weight):
@@ -483,19 +477,19 @@
     vm = pltpu.VMEM
     big = LANES * rows
     scratch = [
-        vm((big, LANES), F32), vm((cols * rows, LANES), F32), vm((big, LANES), F32), vm((rows, LANES), F32),
+        vm((big, LANES), F32), vm((cols * rows, LANES), F32), vm((big, LANES), F32), vm((nt, ext - 4, rows, LANES), F32),
         vm((1, LANES, nobs), F32), vm((cols * rows, LANES), F32),
         vm((nt + 2, tiles, rows, LANES), BF16), vm((nt + 2, tiles, rows, LANES), BF16),
         vm((nt, tiles, rows, LANES), BF16), vm((nt, tiles, rows, LANES), BF16),
         vm((nt, 3, rows, LANES), BF16), vm((nt, 3, rows, LANES), BF16),
         vm((nt + 2, ext, rows, LANES), F32), vm((nt, ext, rows, LANES), F32),
-        vm((ext, rows, 3 * wide), BF16), vm((ext * rows, wide), F32), vm((ext, rows, 3 * hid), BF16),
+        vm((ext, rows, 3 * wide), BF16), vm((nt + 2, (ext - 4) * rows, wide), F32), vm((ext, rows, 3 * hid), BF16),
         vm((nt + 2, ext - 4, rows, LANES), F32),
-        vm((STEPS, nt, mt, rows, LANES), BF16), vm((STEPS, nt, mt, rows, LANES), BF16),
+        vm((nt, mt, rows, LANES), BF16), vm((nt, mt, rows, LANES), BF16),
         vm((cols * rows, LANES), F32),
         vm((STEPS, nt, 8, LANES), F32), vm((STEPS, 2, 8, LANES), F32), vm((STEPS, nl, 8, LANES), F32),
         dma((nt,)), dma((nt,)), dma((nt,)), dma((nt,)), dma((2, 2)), dma((nt,)), dma((nt,)),
-        dma((STEPS, nt)), dma((STEPS, nt)),
+        dma((nt,)), dma((nt,)),
         dma((STEPS, nt)), dma((STEPS, nt)), dma((STEPS, nl)), dma((STEPS, nl)),
         vm((wide, 9 * hid), BF16), vm((9 * wide, hid), BF16), vm((9 * hid, wide), BF16),
     ]

time: 80.7 us -> 69.3 us (0.86)
  Pallas kernels: 78.6 us -> 67.1 us
    pallas_call x1, Pallas kernels: 78.6 us -> 67.1 us  [body(): pl.pallas_call(functools.partial(kernel, nt, nl, nvar, rows, cols, hid),...]
where the time goes in v3:
time: 69.3 us; the launch traced here: 69.1 us
  Pallas kernels  67.1 us (97%)
  local copies, waits for them, and re-layouts  1.95 us (3%)
    pallas_call x1, Pallas kernels, body(): pl.pallas_call(functools.partial(kernel, nt, nl, nvar, rows, cols, hid),...  67.1 us
    unnamed x1, local copies, waits for them, and re-layouts  1.95 us

profile of v3, /device:TPU:0, one launch (start us, length us, event | category | flops | bytes accessed | tf_op | source)
XLA Modules:
  0.0 69.1 jit_solution(10393577076083280554)
XLA Ops:
  0.0 67.1 %shard_map.64 = f32[1248,128]{1,0:T(8,128)} custom-call(f32[1248,128]{1,0:T(8,128)} %bitcast.7, s32[1,256]{1,0:T(1,128)} %loc_ref.1, f32[78,1,256]{2,1,0:T(1,128)} %bitcast.8, bf16[2106,256]{1,0:T(8,128)(2,1)} %bitcast.6, f32[1,256]{1,0:T(1,128)} %bitcast.9, bf16[234,2304]{1,0:T(8,128)(2,1)} %w2_ref.1), custom_call_target="tpu_custom_call" | custom-call | tf_op jit(solution)/shard_map/pallas_call | solution.py:496
  67.1 2.0 %copy.8 = f32[1,78,16,128]{3,2,1,0:T(8,128)} copy(f32[1,78,16,128]{3,2,1,0:T(8,128)} %bitcast.5) | data formatting | bytes 1277952

commit v4 on v3

--- a/solution.py
+++ b/solution.py
@@ -332,21 +332,22 @@
                 def _():
                     arrive(nth(i + 1))
 
-            def window(j, k):
-                c = j * GROUP
+            def window(c):
                 before, here, after = [flat(nu[s + i, pl.ds(c, GROUP)]) for i in range(3)]
                 lane = lane_of(here.shape)
                 moved = turned(here, nvar)
                 first = jnp.where(lane < nvar, before, moved)
                 last = jnp.where(lane < two, moved, jnp.where(lane < two + nvar, turned(after, two), 0.0))
                 spread(x3, c, [first, last])
-                return k
-
-            lax.fori_loop(0, width // GROUP, window, 0, unroll=2)
+
+            built = 0
             wid = width - 2
             bias = b1_ref[...]
             chunk = wid // 2
             for start in range(0, wid, chunk):
+                while built < start + chunk + 2:
+                    window(built)
+                    built += GROUP
                 lhs = jnp.concatenate(
                     [x3[start + k : start + k + chunk].reshape(chunk * rows, 3 * wide) for k in range(3)], 1)
                 whole = jnp.dot(lhs, w1s[...], preferred_element_type=F32)
@@ -358,9 +359,12 @@
                     v = v.astype(BF16).astype(F32)
                     spread(h3, start + c, [v[:, m * LANES : (m + 1) * LANES] for m in range(hid // LANES)])
             wid = width - 4
-            lhs = jnp.concatenate(
-                [h3[k : k + wid].reshape(wid * rows, 3 * hid) for k in range(3)], 1)
-            acc[s + 1, 0 : wid * rows, :] = jnp.dot(lhs, w2s[...], preferred_element_type=F32)
+            chunk = wid // 2
+            for start in range(0, wid, chunk):
+                lhs = jnp.concatenate(
+                    [h3[start + k : start + k + chunk].reshape(chunk * rows, 3 * hid) for k in range(3)], 1)
+                acc[s + 1, start * rows : (start + chunk) * rows, :] = jnp.dot(
+                    lhs, w2s[...], preferred_element_type=F32)
 
             @pl.when(i > 0)
             def _():

time: 69.3 us -> 66.4 us (0.958)
  Pallas kernels: 67.1 us -> 64.2 us
    pallas_call x1, Pallas kernels: 67.1 us -> 64.2 us  [body(): pl.pallas_call(functools.partial(kernel, nt, nl, nvar, rows, cols, hid),...]
where the time goes in v4:
time: 66.4 us; the launch traced here: 66.2 us
  Pallas kernels  64.2 us (97%)
  local copies, waits for them, and re-layouts  1.95 us (3%)
    pallas_call x1, Pallas kernels, body(): pl.pallas_call(functools.partial(kernel, nt, nl, nvar, rows, cols, hid),...  64.2 us
    unnamed x1, local copies, waits for them, and re-layouts  1.95 us

profile of v4, /device:TPU:0, one launch (start us, length us, event | category | flops | bytes accessed | tf_op | source)
XLA Modules:
  0.0 66.2 jit_solution(9521217081477902980)
XLA Ops:
  0.0 64.2 %shard_map.64 = f32[1248,128]{1,0:T(8,128)} custom-call(f32[1248,128]{1,0:T(8,128)} %bitcast.7, s32[1,256]{1,0:T(1,128)} %loc_ref.1, f32[78,1,256]{2,1,0:T(1,128)} %bitcast.8, bf16[2106,256]{1,0:T(8,128)(2,1)} %bitcast.6, f32[1,256]{1,0:T(1,128)} %bitcast.9, bf16[234,2304]{1,0:T(8,128)(2,1)} %w2_ref.1), custom_call_target="tpu_custom_call" | custom-call | tf_op jit(solution)/shard_map/pallas_call | solution.py:500
  64.2 2.0 %copy.8 = f32[1,78,16,128]{3,2,1,0:T(8,128)} copy(f32[1,78,16,128]{3,2,1,0:T(8,128)} %bitcast.5) | data formatting | bytes 1277952
